TPU v7x, 256 devices: a whole 4x4x8 slice. The times are simulated.
256 devices in a mesh: song: 4 (over y), seq: 64 (over z, x, core).
Axes of the slice: x: 4, y: 4, z: 8, core: 2. Of those that a mesh axis runs over, the one named last changes fastest.
Arguments:
- queries: bfloat16 [4, 8192, 2048], P('song', 'seq'), may hold values from -64 to 64
- keys: bfloat16 [4, 8192, 2048], P('song', 'seq'), may hold values from -64 to 64
- values: bfloat16 [4, 8192, 2048], P('song', 'seq'), may hold values from -6 to 6
- lyric_keys: bfloat16 [4, 384, 2048], P('song', 'seq'), may hold values from -64 to 64
- lyric_values: bfloat16 [4, 384, 2048], P('song', 'seq'), may hold values from -6 to 6
- q_gain: float32 [128], replicated, may hold values from 0.5 to 1.5
- k_gain: float32 [128], replicated, may hold values from 0.5 to 1.5
- cotangent: bfloat16 [4, 8192, 2048], P('song', 'seq'), may hold values from -12 to 12
- alignment: int32 [4, 64, 2], P('song', 'seq'), may hold values from -1 to 2, as said below
- lyric_len: int32 [4], P('song'), may hold values from 192 to 384
Outputs:
- attn_out: bfloat16 [4, 8192, 2048], P('song', 'seq')
- grad_queries: bfloat16 [4, 8192, 2048], P('song', 'seq')
- grad_keys: bfloat16 [4, 8192, 2048], P('song', 'seq')
- grad_values: bfloat16 [4, 8192, 2048], P('song', 'seq')
- grad_lyric_keys: bfloat16 [4, 384, 2048], P('song', 'seq')
- grad_lyric_values: bfloat16 [4, 384, 2048], P('song', 'seq')
- grad_q_gain: float32 [128], replicated
- grad_k_gain: float32 [128], replicated
Inputs may be any that keep to these rules, and one draw needn't show every extreme that they name: `alignment`: in each row the entries that are not -1 are distinct.
All inputs are finite; a program needn't handle non-finite values.
Results may differ from a plain program's by a relative error of at most 0.01.
Values may be sent and summed in bfloat16 or wider, within the bound.
A program may use at most 128 MiB of HBM per device.

v0:
```python
import jax
import jax.numpy as jnp
from jax import lax
from jax.sharding import PartitionSpec as P

BLK = 128
WIN = 1
TILES = 2


NORM_EPS = 1e-06


def extended_2(block, sides, width):
    for axis, dim in sides:
        count = lax.axis_size(axis)
        forward = [(i, i + 1) for i in range(count - 1)]
        backward = [(target, source) for source, target in forward]
        low = lax.ppermute(
            lax.slice_in_dim(block, block.shape[dim] - width, None, axis=dim), axis, forward
        )
        high = lax.ppermute(lax.slice_in_dim(block, 0, width, axis=dim), axis, backward)
        block = jnp.concatenate([low, block, high], axis=dim)
    return block


def norm_heads(inputs, norm_gain):
    row_values = inputs.astype(jnp.float32).reshape(inputs.shape[0], -1, norm_gain.shape[0])
    inverse = lax.rsqrt(jnp.mean(row_values * row_values, axis=-1, keepdims=True) + NORM_EPS)
    return (row_values * inverse * norm_gain, inverse)


def norm_back(inputs, inverse, norm_gain, grad_out):
    row_values = inputs.astype(jnp.float32).reshape(grad_out.shape)
    scaled = grad_out * norm_gain
    grad_input = inverse * scaled - row_values * inverse * inverse * inverse * jnp.mean(
        scaled * row_values, axis=-1, keepdims=True
    )
    grad_gain = jnp.sum(grad_out * row_values * inverse, axis=(0, 1))
    return (grad_input.reshape(inputs.shape), grad_gain)


def block_pass(query_rows, key_rows, value_rows, keep_mask, grad_rows, score_scale):
    scores = (
        jnp.einsum("qhd,khd->hqk", query_rows, key_rows, preferred_element_type=jnp.float32)
        * score_scale
    )
    exp_scores = jnp.where(keep_mask[None, None, :], jnp.exp(scores), 0.0)
    totals = jnp.sum(exp_scores, axis=2)
    prob_full = exp_scores / totals[:, :, None]
    prob_low = prob_full.astype(jnp.bfloat16)
    block_output = jnp.einsum(
        "hqk,khd->qhd", prob_low, value_rows, preferred_element_type=jnp.float32
    ).astype(jnp.bfloat16)
    delta_rows = jnp.sum(grad_rows.astype(jnp.float32) * block_output.astype(jnp.float32), axis=2).T
    grad_prob = jnp.einsum(
        "qhd,khd->hqk", grad_rows, value_rows, preferred_element_type=jnp.float32
    )
    grad_score = (prob_full * (grad_prob - delta_rows[:, :, None])).astype(jnp.bfloat16)
    query_gradient = (
        jnp.einsum("hqk,khd->qhd", grad_score, key_rows, preferred_element_type=jnp.float32)
        * score_scale
    )
    grad_key = (
        jnp.einsum("hqk,qhd->khd", grad_score, query_rows, preferred_element_type=jnp.float32)
        * score_scale
    )
    value_gradient = jnp.einsum(
        "hqk,qhd->khd", prob_low, grad_rows, preferred_element_type=jnp.float32
    )
    return (block_output, query_gradient, grad_key, value_gradient, totals, delta_rows)


def body(
    queries, keys, values, lyric_keys, lyric_values, q_gain, k_gain, cotangent, alignment, lyric_len
):
    head_size = q_gain.shape[0]
    model_width = queries.shape[2]
    head_count = model_width // head_size
    frames = queries.shape[1]
    lyric_local = lyric_keys.shape[1]
    blocks = frames // BLK
    border_rows = WIN * BLK
    window_extent = (2 * WIN + 1) * BLK
    score_scale = head_size ** (-0.5)
    total_frames = frames * lax.axis_size("seq")
    first_frame = lax.axis_index("seq") * frames
    query_raw = queries[0]
    key_raw = keys[0]
    query_full, query_inv = norm_heads(query_raw, q_gain)
    key_full, key_inv = norm_heads(key_raw, k_gain)
    lyric_full, lyric_inv = norm_heads(lyric_keys[0], k_gain)
    query_norm = query_full.astype(jnp.bfloat16)
    key_norm = key_full.astype(jnp.bfloat16)
    lyric_norm = lyric_full.astype(jnp.bfloat16)
    lyric_key_all, lyric_val_all = (
        lax.all_gather(lyric_norm.reshape(lyric_local, model_width), "seq", axis=0, tiled=True),
        lax.all_gather(lyric_values[0], "seq", axis=0, tiled=True),
    )
    lyric_total = lyric_key_all.shape[0]
    lyric_key_all = lyric_key_all.reshape(lyric_total, head_count, head_size)
    lyric_val_all = lyric_val_all.reshape(lyric_total, head_count, head_size)
    stacked = jnp.stack([key_norm.reshape(frames, model_width), values[0]])
    extended = extended_2(stacked, (("seq", 1),), border_rows)
    ext_keys = extended[0].reshape(frames + 2 * border_rows, head_count, head_size)
    ext_vals = extended[1].reshape(frames + 2 * border_rows, head_count, head_size)
    grad_heads = cotangent[0].reshape(frames, head_count, head_size)
    length = lyric_len[0]

    def one_block(block_id):
        start_offset = block_id * BLK
        position = (
            first_frame + start_offset - border_rows + jnp.arange(window_extent, dtype=jnp.int32)
        )
        audio_mask = (position >= 0) & (position < total_frames)
        tile_ids = alignment[0, block_id]
        row_grid = (jnp.maximum(tile_ids, 0) * BLK)[:, None] + jnp.arange(BLK, dtype=jnp.int32)[
            None, :
        ]
        lyric_mask = ((tile_ids >= 0)[:, None] & (row_grid < length)).reshape(-1)
        row_index = row_grid.reshape(-1)
        all_keys = jnp.concatenate([ext_keys, jnp.take(lyric_key_all, row_index, axis=0)], axis=0)
        all_vals = jnp.concatenate([ext_vals, jnp.take(lyric_val_all, row_index, axis=0)], axis=0)
        keep_mask = jnp.concatenate([audio_mask, lyric_mask], axis=0)
        results = block_pass(query_norm, all_keys, all_vals, keep_mask, grad_heads, score_scale)
        return results + (row_index,)

    output_list, grad_qn, grad_key, value_gradient, totals, delta_rows, row_index = lax.map(
        one_block, jnp.arange(blocks, dtype=jnp.int32)
    )
    audio_cols = grad_key.shape[1] - TILES * BLK
    flat_rows = row_index.reshape(-1)
    lyric_grad_key = (
        jnp.zeros((lyric_total, head_count, head_size), jnp.float32)
        .at[flat_rows]
        .add(grad_key[:, audio_cols:].reshape(-1, head_count, head_size))
    )
    lyric_grad_val = (
        jnp.zeros((lyric_total, head_count, head_size), jnp.float32)
        .at[flat_rows]
        .add(value_gradient[:, audio_cols:].reshape(-1, head_count, head_size))
    )
    ext_grad_key = jnp.zeros((frames + 2 * border_rows, head_count, head_size), jnp.float32)
    ext_grad_val = jnp.zeros((frames + 2 * border_rows, head_count, head_size), jnp.float32)
    block_id = 0
    lower = block_id * BLK
    ext_grad_key = ext_grad_key.at[lower : lower + window_extent].add(
        grad_key[block_id, :window_extent]
    )
    ext_grad_val = ext_grad_val.at[lower : lower + window_extent].add(
        value_gradient[block_id, :window_extent]
    )
    own_grad_key = ext_grad_key[border_rows : border_rows + frames]
    own_grad_val = ext_grad_val[border_rows : border_rows + frames]
    rims = jnp.stack(
        [
            jnp.concatenate(
                [ext_grad_key[:border_rows], ext_grad_key[border_rows + frames :]], axis=0
            ).reshape(2 * border_rows, model_width),
            jnp.concatenate(
                [ext_grad_val[:border_rows], ext_grad_val[border_rows + frames :]], axis=0
            ).reshape(2 * border_rows, model_width),
        ]
    )
    received = extended_2(rims.astype(jnp.bfloat16), (("seq", 1),), border_rows).astype(rims.dtype)
    from_left = received[:, :border_rows].reshape(2, border_rows, head_count, head_size)
    from_right = received[:, 3 * border_rows :].reshape(2, border_rows, head_count, head_size)
    own_grad_key = (
        own_grad_key.at[:border_rows]
        .add(from_left[0])
        .at[frames - border_rows :]
        .add(from_right[0])
    )
    own_grad_val = (
        own_grad_val.at[:border_rows]
        .add(from_left[1])
        .at[frames - border_rows :]
        .add(from_right[1])
    )
    unnormed_query_gradient, query_gain_vector = norm_back(
        query_raw, query_inv, q_gain, grad_qn.reshape(frames, head_count, head_size)
    )
    unnormed_key_gradient, key_gain_vector = norm_back(key_raw, key_inv, k_gain, own_grad_key)
    summed_key, summed_val = (
        lax.psum_scatter(
            lyric_grad_key.reshape(lyric_total, model_width), "seq", scatter_dimension=0, tiled=True
        ),
        lax.psum_scatter(
            lyric_grad_val.reshape(lyric_total, model_width), "seq", scatter_dimension=0, tiled=True
        ),
    )
    unnormed_lyric_gradient, lyric_gain_vector = norm_back(
        lyric_keys[0], lyric_inv, k_gain, summed_key.reshape(lyric_local, head_count, head_size)
    )
    total_query_gain, total_key_gain = lax.psum(
        (query_gain_vector, key_gain_vector + lyric_gain_vector), ("song", "seq")
    )
    return (
        output_list.reshape(1, frames, model_width),
        unnormed_query_gradient.astype(jnp.bfloat16)[None],
        unnormed_key_gradient.astype(jnp.bfloat16)[None],
        own_grad_val.reshape(1, frames, model_width).astype(jnp.bfloat16),
        unnormed_lyric_gradient.astype(jnp.bfloat16)[None],
        summed_val.astype(jnp.bfloat16)[None],
        total_query_gain,
        total_key_gain,
    )


def solution(mesh):
    in_specs = (
        P("song", "seq", None),
        P("song", "seq", None),
        P("song", "seq", None),
        P("song", "seq", None),
        P("song", "seq", None),
        P(),
        P(),
        P("song", "seq", None),
        P("song", "seq", None),
        P("song"),
    )
    out_specs = (
        P("song", "seq", None),
        P("song", "seq", None),
        P("song", "seq", None),
        P("song", "seq", None),
        P("song", "seq", None),
        P("song", "seq", None),
        P(),
        P(),
    )
    return jax.shard_map(body, mesh=mesh, in_specs=in_specs, out_specs=out_specs, check_vma=False)
```

profile of v0, /device:TPU:16, one launch (start us, length us, event | category | flops | bytes accessed | tf_op | source)
XLA Modules:
  0.0 651.7 jit_solution(4677205366677550377)
XLA Ops:
  17.5 4.0 collective-permute-start
  31.1 61.4 %all-gather.5.cloned.1.call-done = bf16[1,384,2048]{2,0,1:T(2,128)(2,1)} async-done(((bf16[1,6,2048]{2,0,1:T(2,128)(2,1)}), bf16[1,384,2048]{2,0,1:T(2,128)(2,1)}) %all-gather.5.cloned.1.call-update) | async-done | bytes 1572880 | tf_op jit(solution)/shard_map/all_gather | solution.py:98
  92.5 6.9 %copy.100 = bf16[1,384,2048]{1,2,0:T(8,128)(2,1)S(1)} copy(bf16[1,384,2048]{2,0,1:T(2,128)(2,1)} %all-gather.5.cloned.1.call-done) | data formatting | bytes 3145728 | tf_op jit(solution)/shard_map/all_gather | solution.py:98
  99.4 2.0 copy.101
  101.5 69.1 %all-gather.7.cloned.1.call-done = bf16[64,6,2048]{2,1,0:T(8,128)(2,1)} async-done(((bf16[1,6,2048]{2,1,0:T(8,128)(2,1)}), bf16[64,6,2048]{2,1,0:T(8,128)(2,1)}) %all-gather.7.cloned.1.call-update) | async-done | bytes 1572880 | tf_op jit(solution)/shard_map/all_gather | solution.py:97
  170.6 4.4 reshape.472
  174.9 3.2 gather_fusion.1
  184.9 3.1 fusion.56
  188.0 2.4 multiply_reduce_fusion
  195.3 2.1 fusion.55
  198.7 4.1 collective-permute-start.2
  205.2 20.2 %scatter_fusion = f32[384,16,128]{2,1,0:T(8,128)S(1)} fusion(f32[384,16,128]{2,1,0:T(8,128)S(1)} %broadcast.403.clone, s32[256]{0:T(256)S(1)} %bitcast.227, f32[256,16,128]{2,1,0:T(8,128)} %copy.112), kind=kCustom, calls=%fused_computation.2 | custom fusion | flops 524288 | bytes 6292480 | tf_op jit(solution)/shard_map/scatter-add | solution.py:136
  225.4 3.1 copy.146
  230.3 2.0 copy.113
  232.5 20.2 %scatter_fusion.1 = f32[384,16,128]{2,1,0:T(8,128)S(1)} fusion(f32[384,16,128]{2,1,0:T(8,128)S(1)} %broadcast.403.clone.1, s32[256]{0:T(256)S(1)} %bitcast.228, f32[256,16,128]{2,1,0:T(8,128)} %copy.113), kind=kCustom, calls=%fused_computation.3 | custom fusion | flops 524288 | bytes 6292480 | tf_op jit(solution)/shard_map/scatter-add | solution.py:141
  252.8 3.1 copy.145
  255.8 283.9 %all-reduce.7 = bf16[384,2048]{1,0:T(8,128)(2,1)} all-reduce(f32[384,2048]{1,0:T(8,128)} %bitcast.203), channel_id=4, replica_groups=mesh['song'=4,'seq'=64] {'seq'}, use_global_device_ids=true, to_apply=%region_11.13.clone | all-reduce | flops 786432 | bytes 4718592
  539.7 4.1 fusion.18
  545.2 2.4 slice.228
  547.6 2.0 copy.114
  549.7 2.3 fusion.25
  552.0 2.0 copy.115
  560.2 2.0 copy.116
  567.7 77.5 %all-reduce.2 = (f32[128]{0:T(128)}, f32[128]{0:T(128)}) all-reduce(f32[128]{0:T(128)S(1)} %get-tuple-element.214, f32[128]{0:T(128)S(1)} %add.202), channel_id=1, replica_groups=mesh['song'=4,'seq'=64] {'song','seq'}, use_global_device_ids=true, to_apply=%region_13.15 | all-reduce | flops 256 | bytes 2048 | tf_op jit(solution)/shard_map/psum | solution.py:195
  (126 shorter events, 48.3 us)
Async XLA Ops:
  7.2 85.3 %all-gather.5.cloned.1.call-start = ((), (), s32[]{:S(2)}) async-start(), calls=%async_computation | async-start | bytes 3194880 | tf_op jit(solution)/shard_map/all_gather | solution.py:98
  8.7 161.9 %all-gather.7.cloned.1.call-start = ((), (), s32[]{:S(2)}) async-start(), calls=%async_computation.1 | async-start | bytes 2129920 | tf_op jit(solution)/shard_map/all_gather | solution.py:97
  11.7 553.2 %all-reduce.6.cloned.1.call-start = ((), (), s32[]{:S(2)}) async-start(), calls=%async_computation.2 | async-start | bytes 6291456
  13.1 9.1 %copy-start.24 = (s32[1,1,2]{2,1,0:T(1,128)S(1)}, s32[1,1,2]{2,1,0:T(1,128)}, u32[]{:S(2)}) copy-start(s32[1,1,2]{2,1,0:T(1,128)} %param.44) | copy-start | bytes 28
  13.1 9.2 %copy-start.19 = (bf16[1,128,2048]{2,1,0:T(8,128)(2,1)S(1)}, bf16[1,128,2048]{2,1,0:T(8,128)(2,1)}, u32[]{:S(2)}) copy-start(bf16[1,128,2048]{2,1,0:T(8,128)(2,1)} %param.43) | copy-start | bytes 1572868
  14.5 7.8 %copy-start.3 = (bf16[1,128,2048]{1,2,0:T(8,128)(2,1)}, bf16[1,128,2048]{1,2,0:T(8,128)(2,1)S(1)}, u32[]{:S(2)}) copy-start(bf16[1,128,2048]{1,2,0:T(8,128)(2,1)S(1)} %copy.97) | copy-start | bytes 1572868
  15.7 8.9 %copy-start.25 = (u32[256]{0:T(256)S(1)}, u32[256]{0:T(256)}, u32[]{:S(2)}) copy-start(u32[256]{0:T(256)} %constant.274) | copy-start | bytes 3076
  16.1 10.0 %copy-start.23 = (f32[128]{0:T(128)S(1)}, f32[128]{0:T(128)}, u32[]{:S(2)}) copy-start(f32[128]{0:T(128)} %param.41) | copy-start | bytes 1540
  16.2 10.0 %collective-permute-start.1 = (bf16[2,128,2048]{1,2,0:T(8,128)(2,1)S(1)}, bf16[2,128,2048]{1,2,0:T(8,128)(2,1)}, u32[]{:S(2)}, u32[]{:S(2)}) collective-permute-start(bf16[2,128,2048]{1,2,0:T(8,128)(2,1)S(1)} %pad_maximum_fusion.9), channel_id=1, source_target_pairs={{1,0},{2,1},{3,2},{4,3},{5,4},{6,5},{7,6},{8,7},{9,8},{10,9},{11,1... | collective-permute-start | bytes 3145736 | tf_op jit(solution)/shard_map/ppermute | solution.py:22
  17.5 8.7 %collective-permute-start = (bf16[2,128,2048]{1,2,0:T(8,128)(2,1)S(1)}, bf16[2,128,2048]{1,2,0:T(8,128)(2,1)}, u32[]{:S(2)}, u32[]{:S(2)}) collective-permute-start(bf16[2,128,2048]{1,2,0:T(8,128)(2,1)S(1)} %pad_maximum_fusion.9), channel_id=1, source_target_pairs={{0,1},{1,2},{2,3},{3,4},{4,5},{5,6},{6,7},{7,8},{8,9},{9,10},{10,1... | collective-permute-start | bytes 3145736 | tf_op jit(solution)/shard_map/ppermute | solution.py:19
  24.6 167.7 %copy-start.1 = (f32[1,128,2048]{1,2,0:T(8,128)}, f32[1,128,2048]{1,2,0:T(8,128)S(1)}, u32[]{:S(2)}) copy-start(f32[1,128,2048]{1,2,0:T(8,128)S(1)} %copy.103) | copy-start | bytes 3145732
  101.5 76.7 %copy-start.12 = (bf16[384,16,128]{2,1,0:T(8,128)(2,1)S(1)}, bf16[384,16,128]{2,1,0:T(8,128)(2,1)}, u32[]{:S(2)}) copy-start(bf16[384,16,128]{2,1,0:T(8,128)(2,1)} %copy.101) | copy-start | bytes 4718596
  184.9 3.1 copy-start.17
  193.8 9.0 %copy-start = (f32[1,640,16,128]{1,3,2,0:T(8,128)}, f32[1,640,16,128]{1,3,2,0:T(8,128)S(1)}, u32[]{:S(2)}) copy-start(f32[1,640,16,128]{1,3,2,0:T(8,128)S(1)} %get-tuple-element.244) | copy-start | bytes 15728644
  194.3 3.1 copy-start.9
  197.5 358.1 %collective-permute-start.3 = (bf16[2,128,2048]{1,2,0:T(8,128)(2,1)}, bf16[2,128,2048]{1,2,0:T(8,128)(2,1)}, u32[]{:S(2)}, u32[]{:S(2)}) collective-permute-start(bf16[2,128,2048]{1,2,0:T(8,128)(2,1)} %get-tuple-element.234), channel_id=1, source_target_pairs={{1,0},{2,1},{3,2},{4,3},{5,4},{6,5},{7,6},{8,7},{9,8},{10,9},{11,1... | collective-permute-start | bytes 3145736 | tf_op jit(solution)/shard_map/ppermute | solution.py:22
  198.7 356.8 %collective-permute-start.2 = (bf16[2,128,2048]{1,2,0:T(8,128)(2,1)}, bf16[2,128,2048]{1,2,0:T(8,128)(2,1)}, u32[]{:S(2)}, u32[]{:S(2)}) collective-permute-start(bf16[2,128,2048]{1,2,0:T(8,128)(2,1)} %get-tuple-element.233), channel_id=1, source_target_pairs={{0,1},{1,2},{2,3},{3,4},{4,5},{5,6},{6,7},{7,8},{8,9},{9,10},{10,1... | collective-permute-start | bytes 3145736 | tf_op jit(solution)/shard_map/ppermute | solution.py:19
  255.8 283.9 %copy-start.2 = (f32[1,128,2048]{1,2,0:T(8,128)S(1)}, f32[1,128,2048]{1,2,0:T(8,128)}, u32[]{:S(2)}) copy-start(f32[1,128,2048]{1,2,0:T(8,128)} %copy-done.1) | copy-start | bytes 3145732
  255.8 283.9 %copy-start.16 = (bf16[384,16,128]{2,0,1:T(8,128)(2,1)S(1)}, bf16[384,16,128]{2,0,1:T(8,128)(2,1)}, u32[]{:S(2)}) copy-start(bf16[384,16,128]{2,0,1:T(8,128)(2,1)} %copy.105) | copy-start | bytes 4718596
  545.2 10.3 %copy-start.4 = (bf16[1,128,2048]{1,2,0:T(8,128)(2,1)S(1)}, bf16[1,128,2048]{1,2,0:T(8,128)(2,1)}, u32[]{:S(2)}) copy-start(bf16[1,128,2048]{1,2,0:T(8,128)(2,1)} %copy-done.3) | copy-start | bytes 1572868
  545.2 10.3 %copy-start.6 = (bf16[1,128,16,128]{1,3,2,0:T(8,128)(2,1)S(1)}, bf16[1,128,16,128]{1,3,2,0:T(8,128)(2,1)}, u32[]{:S(2)}) copy-start(bf16[1,128,16,128]{1,3,2,0:T(8,128)(2,1)} %copy-done.5) | copy-start | bytes 1572868
  558.9 3.3 copy-start.8
  558.9 3.3 copy-start.10
  562.2 3.8 copy-start.21
  (9 other events, 15.5 us)
Sparse Core Ops, SparseCore 0:
  11.3 81.1 all-gather.4
  95.8 74.6 all-gather.6
  228.6 194.6 all-reduce.5
where the time goes:
time: 656 us; the launch traced here: 652 us
  blocking collectives  361 us (55%)
  waiting for transfers between devices  131 us (20%)
  local copies, waits for them, and re-layouts  60.6 us (9%)
  other arithmetic  58.8 us (9%)
  between operations  15.6 us (2%)
  matrix products  14 us (2%)
  starting transfers between devices  10.8 us (2%)
    unnamed x1, blocking collectives  284 us
    psum x1, blocking collectives, body(): lax.psum((query_gain_vector, key_gain_vector + lyric_gain_vector), ('song...  77.5 us
    all_gather x1, waiting for transfers between devices, body(): lax.all_gather(lyric_norm.reshape(lyric_local, model_width), 'seq', axis=...  69.1 us
    all_gather x1, waiting for transfers between devices, body(): lax.all_gather(lyric_values[0], 'seq', axis=0, tiled=True)  61.4 us
    unnamed x66, local copies, waits for them, and re-layouts  21.5 us
    scatter-add x1, other arithmetic, body(): lyric_grad_val = jnp.zeros((lyric_total, head_count, head_size), jnp.floa...  20.2 us
    scatter-add x1, other arithmetic, body(): lyric_grad_key = jnp.zeros((lyric_total, head_count, head_size), jnp.floa...  20.2 us
  transfers between devices with their start and end apart: 7, of which 2 were waited for; matrix products, arithmetic and copies ran while one was open for 16% of the time, Pallas kernels for 0%

commit v1 on v0

--- a/solution.py
+++ b/solution.py
@@ -68,7 +68,7 @@
     value_gradient = jnp.einsum(
         "hqk,qhd->khd", prob_low, grad_rows, preferred_element_type=jnp.float32
     )
-    return (block_output, query_gradient, grad_key, value_gradient, totals, delta_rows)
+    return (block_output, query_gradient, grad_key, value_gradient)
 
 
 def body(
@@ -79,27 +79,30 @@
     head_count = model_width // head_size
     frames = queries.shape[1]
     lyric_local = lyric_keys.shape[1]
-    blocks = frames // BLK
+    seq_count = lax.axis_size("seq")
     border_rows = WIN * BLK
     window_extent = (2 * WIN + 1) * BLK
     score_scale = head_size ** (-0.5)
-    total_frames = frames * lax.axis_size("seq")
+    total_frames = frames * seq_count
     first_frame = lax.axis_index("seq") * frames
+    lyric_total = lyric_local * seq_count
+    lyric_blocks = lyric_total // BLK
+
+    lyric_pair = jnp.stack([lyric_keys[0], lyric_values[0]])
+    lyric_all = lax.all_gather(lyric_pair, "seq", axis=1, tiled=True)
+    lyric_raw_all = lyric_all[0]
+    lyric_val_all = lyric_all[1].reshape(lyric_total, head_count, head_size)
+
     query_raw = queries[0]
     key_raw = keys[0]
     query_full, query_inv = norm_heads(query_raw, q_gain)
     key_full, key_inv = norm_heads(key_raw, k_gain)
-    lyric_full, lyric_inv = norm_heads(lyric_keys[0], k_gain)
+    lyric_full_all, lyric_inv_all = norm_heads(lyric_raw_all, k_gain)
+    lyric_inv = norm_heads(lyric_keys[0], k_gain)[1]
     query_norm = query_full.astype(jnp.bfloat16)
     key_norm = key_full.astype(jnp.bfloat16)
-    lyric_norm = lyric_full.astype(jnp.bfloat16)
-    lyric_key_all, lyric_val_all = (
-        lax.all_gather(lyric_norm.reshape(lyric_local, model_width), "seq", axis=0, tiled=True),
-        lax.all_gather(lyric_values[0], "seq", axis=0, tiled=True),
-    )
-    lyric_total = lyric_key_all.shape[0]
-    lyric_key_all = lyric_key_all.reshape(lyric_total, head_count, head_size)
-    lyric_val_all = lyric_val_all.reshape(lyric_total, head_count, head_size)
+    lyric_key_all = lyric_full_all.astype(jnp.bfloat16)
+
     stacked = jnp.stack([key_norm.reshape(frames, model_width), values[0]])
     extended = extended_2(stacked, (("seq", 1),), border_rows)
     ext_keys = extended[0].reshape(frames + 2 * border_rows, head_count, head_size)
@@ -107,49 +110,41 @@
     grad_heads = cotangent[0].reshape(frames, head_count, head_size)
     length = lyric_len[0]
 
-    def one_block(block_id):
-        start_offset = block_id * BLK
-        position = (
-            first_frame + start_offset - border_rows + jnp.arange(window_extent, dtype=jnp.int32)
-        )
-        audio_mask = (position >= 0) & (position < total_frames)
-        tile_ids = alignment[0, block_id]
-        row_grid = (jnp.maximum(tile_ids, 0) * BLK)[:, None] + jnp.arange(BLK, dtype=jnp.int32)[
-            None, :
-        ]
-        lyric_mask = ((tile_ids >= 0)[:, None] & (row_grid < length)).reshape(-1)
-        row_index = row_grid.reshape(-1)
-        all_keys = jnp.concatenate([ext_keys, jnp.take(lyric_key_all, row_index, axis=0)], axis=0)
-        all_vals = jnp.concatenate([ext_vals, jnp.take(lyric_val_all, row_index, axis=0)], axis=0)
-        keep_mask = jnp.concatenate([audio_mask, lyric_mask], axis=0)
-        results = block_pass(query_norm, all_keys, all_vals, keep_mask, grad_heads, score_scale)
-        return results + (row_index,)
-
-    output_list, grad_qn, grad_key, value_gradient, totals, delta_rows, row_index = lax.map(
-        one_block, jnp.arange(blocks, dtype=jnp.int32)
-    )
-    audio_cols = grad_key.shape[1] - TILES * BLK
-    flat_rows = row_index.reshape(-1)
-    lyric_grad_key = (
-        jnp.zeros((lyric_total, head_count, head_size), jnp.float32)
-        .at[flat_rows]
-        .add(grad_key[:, audio_cols:].reshape(-1, head_count, head_size))
-    )
-    lyric_grad_val = (
-        jnp.zeros((lyric_total, head_count, head_size), jnp.float32)
-        .at[flat_rows]
-        .add(value_gradient[:, audio_cols:].reshape(-1, head_count, head_size))
-    )
-    ext_grad_key = jnp.zeros((frames + 2 * border_rows, head_count, head_size), jnp.float32)
-    ext_grad_val = jnp.zeros((frames + 2 * border_rows, head_count, head_size), jnp.float32)
-    block_id = 0
-    lower = block_id * BLK
-    ext_grad_key = ext_grad_key.at[lower : lower + window_extent].add(
-        grad_key[block_id, :window_extent]
-    )
-    ext_grad_val = ext_grad_val.at[lower : lower + window_extent].add(
-        value_gradient[block_id, :window_extent]
-    )
+    position = first_frame - border_rows + jnp.arange(window_extent, dtype=jnp.int32)
+    audio_mask = (position >= 0) & (position < total_frames)
+    tile_ids = alignment[0, 0]
+    starts = [jnp.maximum(tile_ids[s], 0) * BLK for s in range(TILES)]
+    slot_keys = [lax.dynamic_slice_in_dim(lyric_key_all, st, BLK, 0) for st in starts]
+    slot_vals = [lax.dynamic_slice_in_dim(lyric_val_all, st, BLK, 0) for st in starts]
+    lyric_mask = jnp.concatenate(
+        [(tile_ids[s] >= 0) & (starts[s] + jnp.arange(BLK, dtype=jnp.int32) < length) for s in range(TILES)]
+    )
+    all_keys = jnp.concatenate([ext_keys] + slot_keys, axis=0)
+    all_vals = jnp.concatenate([ext_vals] + slot_vals, axis=0)
+    keep_mask = jnp.concatenate([audio_mask, lyric_mask], axis=0)
+    block_output, grad_qn, grad_key, value_gradient = block_pass(
+        query_norm, all_keys, all_vals, keep_mask, grad_heads, score_scale
+    )
+
+    lyric_gk = grad_key[window_extent:].reshape(TILES, BLK, head_count, head_size)
+    lyric_gv = value_gradient[window_extent:].reshape(TILES, BLK, head_count, head_size)
+    block_ids = jnp.arange(lyric_blocks, dtype=jnp.int32)
+    pick = [(tile_ids[s] == block_ids)[:, None, None, None] for s in range(TILES)]
+    part_gk = sum(jnp.where(pick[s], lyric_gk[s][None], 0.0) for s in range(TILES))
+    part_gv = sum(jnp.where(pick[s], lyric_gv[s][None], 0.0) for s in range(TILES))
+
+    lyric_scaled_all = lyric_raw_all.astype(jnp.float32).reshape(lyric_blocks, BLK, head_count, head_size) * (
+        lyric_inv_all.reshape(lyric_blocks, BLK, head_count, 1)
+    )
+    lyric_gain_vector = jnp.sum(part_gk * lyric_scaled_all, axis=(0, 1, 2))
+
+    parts = jnp.stack([part_gk, part_gv]).reshape(2, seq_count, lyric_local * model_width)
+    summed = lax.psum_scatter(parts, "seq", scatter_dimension=1, tiled=True)
+    summed_key = summed[0].reshape(lyric_local, head_count, head_size)
+    summed_val = summed[1].reshape(lyric_local, model_width)
+
+    ext_grad_key = grad_key[:window_extent]
+    ext_grad_val = value_gradient[:window_extent]
     own_grad_key = ext_grad_key[border_rows : border_rows + frames]
     own_grad_val = ext_grad_val[border_rows : border_rows + frames]
     rims = jnp.stack(
@@ -181,29 +176,19 @@
         query_raw, query_inv, q_gain, grad_qn.reshape(frames, head_count, head_size)
     )
     unnormed_key_gradient, key_gain_vector = norm_back(key_raw, key_inv, k_gain, own_grad_key)
-    summed_key, summed_val = (
-        lax.psum_scatter(
-            lyric_grad_key.reshape(lyric_total, model_width), "seq", scatter_dimension=0, tiled=True
-        ),
-        lax.psum_scatter(
-            lyric_grad_val.reshape(lyric_total, model_width), "seq", scatter_dimension=0, tiled=True
-        ),
-    )
-    unnormed_lyric_gradient, lyric_gain_vector = norm_back(
-        lyric_keys[0], lyric_inv, k_gain, summed_key.reshape(lyric_local, head_count, head_size)
-    )
-    total_query_gain, total_key_gain = lax.psum(
-        (query_gain_vector, key_gain_vector + lyric_gain_vector), ("song", "seq")
-    )
+    total_gains = lax.psum(
+        jnp.stack([query_gain_vector, key_gain_vector + lyric_gain_vector]), ("song", "seq")
+    )
+    unnormed_lyric_gradient = norm_back(lyric_keys[0], lyric_inv, k_gain, summed_key)[0]
     return (
-        output_list.reshape(1, frames, model_width),
+        block_output.reshape(1, frames, model_width),
         unnormed_query_gradient.astype(jnp.bfloat16)[None],
         unnormed_key_gradient.astype(jnp.bfloat16)[None],
         own_grad_val.reshape(1, frames, model_width).astype(jnp.bfloat16),
         unnormed_lyric_gradient.astype(jnp.bfloat16)[None],
         summed_val.astype(jnp.bfloat16)[None],
-        total_query_gain,
-        total_key_gain,
+        total_gains[0],
+        total_gains[1],
     )
 
 

time: 656 us -> 410 us (0.62)
  blocking collectives: 361 us -> 88.5 us
  local copies, waits for them, and re-layouts: 60.6 us -> 91.8 us
  other arithmetic: 58.8 us -> 32.9 us
  waiting for transfers between devices: 131 us -> 151 us
    unnamed x1 -> x0, blocking collectives: 284 us -> none
    unnamed x4 -> x3, waiting for transfers between devices: 0.05 us -> 89.8 us
    all_gather x2 -> x1, waiting for transfers between devices: 130 us -> 61.2 us  [body(): lyric_all = lax.all_gather(lyric_pair, 'seq', axis=1, tiled=True)]
    scatter-add x2 -> x0, other arithmetic: 40.5 us -> none  [the longest x1 20.2 us: body(): lyric_grad_val = jnp.zeros((lyric_total, head_count, head_size), jnp.floa...]
    slice x3 -> x10, local copies, waits for them, and re-layouts: 5.83 us -> 27.2 us  [the longest x1 9.57 us: body(): lyric_raw_all = lyric_all[0]]
    broadcast_in_dim x1 -> x8, local copies, waits for them, and re-layouts: 1.47 us -> 15 us  [body(): jnp.where(pick[s], lyric_gk[s][None], 0.0)]
    reshape x6 -> x0, local copies, waits for them, and re-layouts: 12.4 us -> none  [the longest x1 4.37 us: body(): lyric_key_all = lyric_key_all.reshape(lyric_total, head_count, head_size)]
    psum x1, blocking collectives: 77.5 us -> 88.5 us  [body(): lax.psum(jnp.stack([query_gain_vector, key_gain_vector + lyric_gain_vecto...]
  transfers between devices with their start and end apart: 7 -> 6, of which waited for: 2 -> 2; matrix products, arithmetic and copies ran while one was open for 16% -> 12% of each run, Pallas kernels for 0% -> 0%
where the time goes in v1:
time: 410 us; the launch traced here: 409 us
  waiting for transfers between devices  151 us (37%)
  local copies, waits for them, and re-layouts  91.8 us (22%)
  blocking collectives  88.5 us (22%)
  other arithmetic  32.9 us (8%)
  between operations  17.9 us (4%)
  matrix products  15.8 us (4%)
  starting transfers between devices  10.7 us (3%)
    unnamed x3, waiting for transfers between devices  89.8 us
    psum x1, blocking collectives, body(): lax.psum(jnp.stack([query_gain_vector, key_gain_vector + lyric_gain_vecto...  88.5 us
    all_gather x1, waiting for transfers between devices, body(): lyric_all = lax.all_gather(lyric_pair, 'seq', axis=1, tiled=True)  61.2 us
    unnamed x59, local copies, waits for them, and re-layouts  19.6 us
    broadcast_in_dim x8, local copies, waits for them, and re-layouts, body(): jnp.where(pick[s], lyric_gk[s][None], 0.0)  15 us
    slice x1, local copies, waits for them, and re-layouts, body(): lyric_raw_all = lyric_all[0]  9.57 us
  transfers between devices with their start and end apart: 6, of which 2 were waited for; matrix products, arithmetic and copies ran while one was open for 12% of the time, Pallas kernels for 0%

profile of v1, /device:TPU:16, one launch (start us, length us, event | category | flops | bytes accessed | tf_op | source)
XLA Modules:
  0.0 408.6 jit_solution(17352905032902719818)
XLA Ops:
  15.9 4.0 collective-permute-start
  31.3 61.2 %all-gather.2.cloned.1.call-done = bf16[2,384,2048]{2,0,1:T(2,128)(2,1)} async-done(((bf16[2,6,2048]{2,0,1:T(2,128)(2,1)}), bf16[2,384,2048]{2,0,1:T(2,128)(2,1)}) %all-gather.2.cloned.1.call-update) | async-done | bytes 3145744 | tf_op jit(solution)/shard_map/all_gather | solution.py:92
  92.5 9.6 %fusion.43 = (bf16[1,384,2048]{2,0,1:T(2,128)(2,1)}, bf16[1,384,2048]{2,0,1:T(2,128)(2,1)}) fusion(bf16[2,384,2048]{2,0,1:T(2,128)(2,1)} %all-gather.2.cloned.1.call-done), kind=kLoop, calls=%fused_computation.109 | loop fusion | bytes 6291456 | tf_op jit(solution)/shard_map/slice | solution.py:93
  102.1 6.9 %copy.192 = bf16[1,384,2048]{1,2,0:T(8,128)(2,1)S(1)} copy(bf16[1,384,2048]{2,0,1:T(2,128)(2,1)} %get-tuple-element.169) | data formatting | bytes 3145728
  111.5 6.9 %copy.162 = bf16[1,384,2048]{1,2,0:T(8,128)(2,1)S(1)} copy(bf16[1,384,2048]{2,0,1:T(2,128)(2,1)} %get-tuple-element.170) | data formatting | bytes 3145728 | tf_op jit(solution)/shard_map/slice | solution.py:94
  118.4 2.4 multiply_convert_fusion
  124.3 3.1 fusion.48
  127.4 2.4 multiply_reduce_fusion.4
  132.0 3.3 fusion.47
  139.2 4.0 collective-permute-start.2
  145.2 3.3 maximum_convert_fusion
  153.3 3.7 fusion.41
  159.9 4.5 %select_add_fusion.1 = (f32[3,128,16,128]{3,2,1,0:T(8,128)S(1)}, f32[3,128,16,128]{3,2,1,0:T(8,128)}) fusion(f32[128,16,128]{2,1,0:T(8,128)} %copy.174, f32[128,16,128]{2,1,0:T(8,128)} %copy.173, pred[3]{0:T(512)(128)(4,1)S(1)} %get-tuple-element.198, pred[3]{0:T(512)(128)(4,1)S(1)} %get-tuple-element.199, f32[128,16,128]{2,1,0:T(8,128)} %copy.176, ...), kind=kLoop, calls=%fused_computation.10 | loop fusion | flops 4718592 | bytes 10485766 | tf_op jit(solution)/shard_map/add | solution.py:133
  164.4 4.3 %add.181 = f32[1,64,12288]{2,1,0:T(8,128)} reshape(f32[3,128,16,128]{3,2,1,0:T(8,128)} %get-tuple-element.184) | data formatting | bytes 6291456 | tf_op jit(solution)/shard_map/add | solution.py:134
  170.6 3.3 pad_maximum_fusion
  173.9 7.5 %copy.177 = f32[2,64,12288]{2,0,1:T(2,128)} copy(f32[2,64,12288]{2,1,0:T(8,128)S(1)} %pad_maximum_fusion) | data formatting | bytes 12582912 | tf_op jit(solution)/shard_map/stack | solution.py:141
  183.5 3.2 fusion.16
  191.3 3.7 copy.181
  201.1 3.5 copy.179
  206.1 2.3 broadcast_in_dim.113
  208.5 3.7 copy.178
  212.1 4.6 %multiply_reduce_fusion = f32[2048]{0:T(1024)S(1)} fusion(f32[1,384,2048]{1,2,0:T(8,128)} %copy.181, f32[1,384,2048]{1,2,0:T(8,128)} %copy.179, f32[1,384,2048]{1,2,0:T(8,128)} %copy.178, pred[384]{0:T(512)(128)(4,1)S(1)} %broadcast_bitcast_fusion.1, pred[384]{0:T(512)(128)(4,1)S(1)} %broadcast_bitcast_fusion.2, bf16[1,384,2048]{1,2,0:T(8,128)(2,1)S(1)} %copy-done.1), kind=kLoop, calls=%fused_computation.8 | loop fusion | flops 5502976 | bytes 11019008 | tf_op jit(solution)/shard_map/reduce_sum | solution.py:139
  216.8 88.5 %psum.7 = f32[2,128]{1,0:T(2,128)S(1)} all-reduce(f32[2,128]{1,0:T(2,128)S(1)} %pad_maximum_fusion.16), channel_id=1, replica_groups=mesh['song'=4,'seq'=64] {'song','seq'}, use_global_device_ids=true, to_apply=%region_14.15 | all-reduce | flops 256 | bytes 2048 | tf_op jit(solution)/shard_map/psum | solution.py:179
  305.8 89.8 %all-reduce.3.cloned.1.call-done = f32[2,64,12288]{2,0,1:T(2,128)} async-done(((f32[2,64,12288]{2,0,1:T(2,128)}), f32[2,64,12288]{2,0,1:T(2,128)}) %all-reduce.3.cloned.1.call-update) | async-done | bytes 6291472
  (135 shorter events, 60.9 us)
Async XLA Ops:
  7.2 85.3 %all-gather.2.cloned.1.call-start = ((), (), s32[]{:S(2)}) async-start(), calls=%async_computation | async-start | bytes 3194880 | tf_op jit(solution)/shard_map/all_gather | solution.py:92
  9.6 386.0 %all-reduce.3.cloned.1.call-start = ((), (), s32[]{:S(2)}) async-start(), calls=%async_computation.1 | async-start | bytes 12582912
  10.9 9.0 %copy-start.19 = (s32[1,1,2]{2,1,0:T(1,128)S(1)}, s32[1,1,2]{2,1,0:T(1,128)}, u32[]{:S(2)}) copy-start(s32[1,1,2]{2,1,0:T(1,128)} %param.34) | copy-start | bytes 28
  11.0 12.2 %copy-start.12 = (bf16[1,128,2048]{2,1,0:T(8,128)(2,1)S(1)}, bf16[1,128,2048]{2,1,0:T(8,128)(2,1)}, u32[]{:S(2)}) copy-start(bf16[1,128,2048]{2,1,0:T(8,128)(2,1)} %param.33) | copy-start | bytes 1572868
  14.6 11.6 %collective-permute-start.1 = (bf16[2,128,2048]{1,2,0:T(8,128)(2,1)S(1)}, bf16[2,128,2048]{1,2,0:T(8,128)(2,1)}, u32[]{:S(2)}, u32[]{:S(2)}) collective-permute-start(bf16[2,128,2048]{1,2,0:T(8,128)(2,1)S(1)} %pad_maximum_fusion.9), channel_id=1, source_target_pairs={{1,0},{2,1},{3,2},{4,3},{5,4},{6,5},{7,6},{8,7},{9,8},{10,9},{11,1... | collective-permute-start | bytes 3145736 | tf_op jit(solution)/shard_map/ppermute | solution.py:22
  15.9 10.3 %collective-permute-start = (bf16[2,128,2048]{1,2,0:T(8,128)(2,1)S(1)}, bf16[2,128,2048]{1,2,0:T(8,128)(2,1)}, u32[]{:S(2)}, u32[]{:S(2)}) collective-permute-start(bf16[2,128,2048]{1,2,0:T(8,128)(2,1)S(1)} %pad_maximum_fusion.9), channel_id=1, source_target_pairs={{0,1},{1,2},{2,3},{3,4},{4,5},{5,6},{6,7},{7,8},{8,9},{9,10},{10,1... | collective-permute-start | bytes 3145736 | tf_op jit(solution)/shard_map/ppermute | solution.py:19
  26.0 106.0 %copy-start.2 = (f32[1,128,2048]{1,2,0:T(8,128)}, f32[1,128,2048]{1,2,0:T(8,128)S(1)}, u32[]{:S(2)}) copy-start(f32[1,128,2048]{1,2,0:T(8,128)S(1)} %copy.163) | copy-start | bytes 3145732
  109.0 2.5 copy-start
  111.1 7.3 %copy-start.18 = (f32[128]{0:T(128)S(1)}, f32[128]{0:T(128)}, u32[]{:S(2)}) copy-start(f32[128]{0:T(128)} %param.32) | copy-start | bytes 1540
  121.0 3.2 copy-start.15
  121.0 3.2 copy-start.16
  124.2 3.1 copy-start.11
  132.0 3.3 copy-start.7
  136.0 7.2 %copy-start.21 = (u32[256]{0:T(256)S(1)}, u32[256]{0:T(256)}, u32[]{:S(2)}) copy-start(u32[256]{0:T(256)} %constant.174) | copy-start | bytes 3076
  136.2 12.3 %slice-start = ((s8[5242880]{0:T(1024)(128)(4,1)}), s8[1048576]{0:T(1024)(128)(4,1)S(1)}, s32[]{:S(2)}) async-start(s8[5242880]{0:T(1024)(128)(4,1)} %bitcast.106), calls=%async_computation.2 | async-start | bytes 2097152
  137.9 7.3 %collective-permute-start.3 = (bf16[2,128,2048]{1,2,0:T(8,128)(2,1)}, bf16[2,128,2048]{1,2,0:T(8,128)(2,1)}, u32[]{:S(2)}, u32[]{:S(2)}) collective-permute-start(bf16[2,128,2048]{1,2,0:T(8,128)(2,1)} %get-tuple-element.176), channel_id=1, source_target_pairs={{1,0},{2,1},{3,2},{4,3},{5,4},{6,5},{7,6},{8,7},{9,8},{10,9},{11,1... | collective-permute-start | bytes 3145736 | tf_op jit(solution)/shard_map/ppermute | solution.py:22
  139.2 6.0 %collective-permute-start.2 = (bf16[2,128,2048]{1,2,0:T(8,128)(2,1)}, bf16[2,128,2048]{1,2,0:T(8,128)(2,1)}, u32[]{:S(2)}, u32[]{:S(2)}) collective-permute-start(bf16[2,128,2048]{1,2,0:T(8,128)(2,1)} %get-tuple-element.175), channel_id=1, source_target_pairs={{0,1},{1,2},{2,3},{3,4},{4,5},{5,6},{6,7},{7,8},{8,9},{9,10},{10,1... | collective-permute-start | bytes 3145736 | tf_op jit(solution)/shard_map/ppermute | solution.py:19
  145.2 3.3 slice-start.1
  145.2 3.7 copy-start.4
  181.4 2.1 copy-start.3
  181.4 2.1 copy-start.10
  191.3 3.7 copy-start.5
  191.3 3.7 copy-start.6
  208.5 3.7 copy-start.1
  (6 other events, 8.3 us)
Sparse Core Ops, SparseCore 0:
  11.3 81.1 all-gather.1
  181.5 213.9 all-reduce.2
